TPU v7x, 32 devices: a whole 2x2x4 slice. The times are simulated.
32 devices in a mesh: tm: 2 (over core), loan: 8 (over z, y), cov: 2 (over x).
Axes of the slice: x: 2, y: 2, z: 4, core: 2. Of those that a mesh axis runs over, the one named last changes fastest.
Arguments:
- covars: float32 [65536, 1024], P(('tm', 'loan'), 'cov'), may hold values from -6 to 6
- events: int32 [65536], P(('tm', 'loan')), may hold values 0 or 1
- group: int32 [65536], P(('tm', 'loan')), may hold values from 0 to 511, as said below
- counts: int32 [16], P(('tm', 'loan')), may hold values from 1024 to 4096
- beta: float32 [1024], P('cov'), may hold values from -0.1875 to 0.1875
- vecs: float32 [2, 1024], P(None, 'cov'), may hold values from -12 to 12
Outputs:
- hessvec: float32 [2, 1024], P(None, 'cov')
Inputs may be any that keep to these rules, and one draw needn't show every extreme that they name: `group`: block b holds tie groups of time shard b // (16 // (512 // 256)) only: from 256 times the shard's index to 256 more minus one; the first 256 rows of every block hold each of these groups once.
All inputs are finite; a program needn't handle non-finite values. No bound on the sum of `events` on one device may be relied on, other than what follows from the above.
Results may differ from a plain program's by a relative error of at most 0.00028.
Values sent between devices are 32-bit elements; how exact they have to be, the bound alone decides.
No kernel may reach another device: no remote copies, remote signals or barrier semaphores. Data moves between devices by JAX's collectives and lax.ppermute only.
A program may use at most 64 MiB of HBM per device.

v0:
```python
import jax
import jax.numpy as jnp
from jax import lax
from jax.sharding import PartitionSpec as P

G_SH = 256
exact_mode = lax.Precision.HIGHEST


def carried_in(value, axis, join, neutral, backward):
    count, mine = (lax.axis_size(axis), lax.axis_index(axis))
    pieces = lax.all_gather(value, axis)
    if backward:
        pieces = pieces[::-1]
        mine = count - 1 - mine
    running = jnp.full_like(value, 0) + jnp.asarray(neutral, value.dtype)

    def hop(position, running):
        longer = join(running, pieces[position])
        return jnp.where(position < mine, longer, running)

    return lax.fori_loop(0, count - 1, hop, running)


def add_trees(earlier, later):
    return jax.tree.map(jnp.add, earlier, later)


def sweep(trips, block, update, initial):

    def advance(trip_index, carry):
        return update(trip_index * block, carry)

    return lax.fori_loop(0, trips, advance, initial)


def per_device(covars, events, group, counts, beta, vecs):
    row_total, col_width = covars.shape
    block = min(512, row_total)
    shard = lax.axis_index("tm")
    records_all = row_total * lax.axis_size("tm") * lax.axis_size("loan")
    row_count = counts[0]
    trips = row_total // block
    coeffs = jnp.concatenate([beta[None, :], vecs], axis=0)

    def predict(start, partial_value):
        piece = lax.dynamic_slice_in_dim(covars, start, block, 0)
        values = lax.dot_general(coeffs, piece, (((1,), (1,)), ((), ())), precision=exact_mode)
        return lax.dynamic_update_slice_in_dim(partial_value, values, start, 1)

    partial_value = sweep(trips, block, predict, jnp.zeros((3, row_total), jnp.float32))
    linear = lax.psum(partial_value, "cov")
    valid = (jnp.arange(row_total, dtype=jnp.int32) < row_count).astype(jnp.float32)
    weight = valid * jnp.exp(linear[0])
    projected = linear[1:3]
    died = valid * events.astype(jnp.float32)
    per_record = jnp.concatenate(
        [weight[None, :], weight[None, :] * projected, died[None, :]], axis=0
    )
    local_group = group - shard * G_SH
    group_iota = jnp.arange(G_SH, dtype=jnp.int32)
    upper_ones = (group_iota[:, None] >= group_iota[None, :]).astype(jnp.float32)

    def indicator(start):
        labels = lax.dynamic_slice_in_dim(local_group, start, block, 0)
        return (labels[:, None] == group_iota[None, :]).astype(jnp.float32)

    def tally(start, stats_acc):
        member = indicator(start)
        values = lax.dynamic_slice_in_dim(per_record, start, block, 1)
        return stats_acc + jnp.dot(values, member, precision=exact_mode)

    stats_local = sweep(trips, block, tally, jnp.zeros((4, G_SH), jnp.float32))
    totals = lax.psum(stats_local, "loan")
    sums = totals[:3]
    died_grp = totals[3]
    tail = carried_in(jnp.sum(sums, axis=1), "tm", add_trees, jnp.zeros((3,), jnp.float32), True)
    risk = jnp.dot(sums, upper_ones, precision=exact_mode) + tail[:, None]
    ratios = jnp.concatenate(
        [
            (died_grp / risk[0])[None, :],
            died_grp[None, :] * risk[1:3] / (risk[0] * risk[0])[None, :],
        ],
        axis=0,
    )
    head = carried_in(jnp.sum(ratios, axis=1), "tm", add_trees, jnp.zeros((3,), jnp.float32), False)
    cumulative = jnp.dot(ratios, upper_ones.T, precision=exact_mode) + head[:, None]

    def assemble(start, product_acc):
        member = indicator(start)
        looked = lax.dot_general(cumulative, member, (((1,), (1,)), ((), ())), precision=exact_mode)
        weight_part = lax.dynamic_slice_in_dim(weight, start, block, 0)
        proj_part = lax.dynamic_slice_in_dim(projected, start, block, 1)
        resid = weight_part[None, :] * (proj_part * looked[0][None, :] - looked[1:3])
        piece = lax.dynamic_slice_in_dim(covars, start, block, 0)
        return product_acc + jnp.dot(resid, piece, precision=exact_mode)

    parts = sweep(trips, block, assemble, jnp.zeros((2, col_width), jnp.float32))
    product = lax.psum(parts, ("tm", "loan"))
    return product / records_all


def solution(mesh):
    return jax.shard_map(
        per_device,
        mesh=mesh,
        in_specs=(
            P(("tm", "loan"), "cov"),
            P(("tm", "loan")),
            P(("tm", "loan")),
            P(("tm", "loan")),
            P("cov"),
            P(None, "cov"),
        ),
        out_specs=P(None, "cov"),
        check_vma=False,
    )
```

profile of v0, /device:TPU:0, one launch (start us, length us, event | category | flops | bytes accessed | tf_op | source)
XLA Modules:
  0.0 113.7 jit_solution(10290802062483819432)
XLA Ops:
  0.7 0.7 pad_maximum_fusion.1
  1.4 17.8 %while.51 = (s32[]{:T(128)}, f32[3,4096]{1,0:T(4,128)S(1)}, f32[4096,512]{1,0:T(8,128)}, f32[3,512]{1,0:T(4,128)S(1)}, s32[]{:T(128)}, /*index=5*/s32[]{:T(128)}, s32[]{:T(128)}, s32[]{:T(128)}) while((s32[]{:T(128)}, f32[3,4096]{1,0:T(4,128)S(1)}, f32[4096,512]{1,0:T(8,128)}, f32[3,512]{1,0:T(4,128)S(1)}, s32[]{:T(128)}, ...), condition=%wide.region_1.0_spmd, body=%wide.region_0.0_spmd.sunk | while | flops 9437190 | bytes 1066115 | solution.py:34
  1.4 2.2 %fusion.35 = f32[3,4096]{1,0:T(4,128)S(1)} fusion(f32[3,4096]{1,0:T(4,128)S(1)} %get-tuple-element.532, s32[]{:T(128)S(6)} %select_n.77, f32[3,512]{1,0:T(4,128)S(1)} %get-tuple-element.542, f32[4096,512]{1,0:T(8,128)} %get-tuple-element.541), kind=kOutput, calls=%fused_computation.3.clone.1 | convolution fusion | flops 9437184 | bytes 1065984 | tf_op jit(solution)/shard_map/while/body/eval_jaxpr/dot_general | solution.py:48
  3.6 2.2 %fusion.35 = f32[3,4096]{1,0:T(4,128)S(1)} fusion(f32[3,4096]{1,0:T(4,128)S(1)} %get-tuple-element.532, s32[]{:T(128)S(6)} %select_n.77, f32[3,512]{1,0:T(4,128)S(1)} %get-tuple-element.542, f32[4096,512]{1,0:T(8,128)} %get-tuple-element.541), kind=kOutput, calls=%fused_computation.3.clone.1 | convolution fusion | flops 9437184 | bytes 1065984 | tf_op jit(solution)/shard_map/while/body/eval_jaxpr/dot_general | solution.py:48
  5.8 2.2 %fusion.35 = f32[3,4096]{1,0:T(4,128)S(1)} fusion(f32[3,4096]{1,0:T(4,128)S(1)} %get-tuple-element.532, s32[]{:T(128)S(6)} %select_n.77, f32[3,512]{1,0:T(4,128)S(1)} %get-tuple-element.542, f32[4096,512]{1,0:T(8,128)} %get-tuple-element.541), kind=kOutput, calls=%fused_computation.3.clone.1 | convolution fusion | flops 9437184 | bytes 1065984 | tf_op jit(solution)/shard_map/while/body/eval_jaxpr/dot_general | solution.py:48
  8.0 2.2 %fusion.35 = f32[3,4096]{1,0:T(4,128)S(1)} fusion(f32[3,4096]{1,0:T(4,128)S(1)} %get-tuple-element.532, s32[]{:T(128)S(6)} %select_n.77, f32[3,512]{1,0:T(4,128)S(1)} %get-tuple-element.542, f32[4096,512]{1,0:T(8,128)} %get-tuple-element.541), kind=kOutput, calls=%fused_computation.3.clone.1 | convolution fusion | flops 9437184 | bytes 1065984 | tf_op jit(solution)/shard_map/while/body/eval_jaxpr/dot_general | solution.py:48
  10.3 2.2 %fusion.35 = f32[3,4096]{1,0:T(4,128)S(1)} fusion(f32[3,4096]{1,0:T(4,128)S(1)} %get-tuple-element.532, s32[]{:T(128)S(6)} %select_n.77, f32[3,512]{1,0:T(4,128)S(1)} %get-tuple-element.542, f32[4096,512]{1,0:T(8,128)} %get-tuple-element.541), kind=kOutput, calls=%fused_computation.3.clone.1 | convolution fusion | flops 9437184 | bytes 1065984 | tf_op jit(solution)/shard_map/while/body/eval_jaxpr/dot_general | solution.py:48
  12.5 2.2 %fusion.35 = f32[3,4096]{1,0:T(4,128)S(1)} fusion(f32[3,4096]{1,0:T(4,128)S(1)} %get-tuple-element.532, s32[]{:T(128)S(6)} %select_n.77, f32[3,512]{1,0:T(4,128)S(1)} %get-tuple-element.542, f32[4096,512]{1,0:T(8,128)} %get-tuple-element.541), kind=kOutput, calls=%fused_computation.3.clone.1 | convolution fusion | flops 9437184 | bytes 1065984 | tf_op jit(solution)/shard_map/while/body/eval_jaxpr/dot_general | solution.py:48
  14.7 2.2 %fusion.35 = f32[3,4096]{1,0:T(4,128)S(1)} fusion(f32[3,4096]{1,0:T(4,128)S(1)} %get-tuple-element.532, s32[]{:T(128)S(6)} %select_n.77, f32[3,512]{1,0:T(4,128)S(1)} %get-tuple-element.542, f32[4096,512]{1,0:T(8,128)} %get-tuple-element.541), kind=kOutput, calls=%fused_computation.3.clone.1 | convolution fusion | flops 9437184 | bytes 1065984 | tf_op jit(solution)/shard_map/while/body/eval_jaxpr/dot_general | solution.py:48
  16.9 2.2 %fusion.35 = f32[3,4096]{1,0:T(4,128)S(1)} fusion(f32[3,4096]{1,0:T(4,128)S(1)} %get-tuple-element.532, s32[]{:T(128)S(6)} %select_n.77, f32[3,512]{1,0:T(4,128)S(1)} %get-tuple-element.542, f32[4096,512]{1,0:T(8,128)} %get-tuple-element.541), kind=kOutput, calls=%fused_computation.3.clone.1 | convolution fusion | flops 9437184 | bytes 1065984 | tf_op jit(solution)/shard_map/while/body/eval_jaxpr/dot_general | solution.py:48
  19.1 10.4 %psum.21 = f32[3,4096]{1,0:T(4,128)S(1)} all-reduce(f32[3,4096]{1,0:T(4,128)S(1)} %get-tuple-element.347), channel_id=1, replica_groups=mesh['tm'=2,'loan'=8,'cov'=2] {'cov'}, use_global_device_ids=true, to_apply=%region_2.0 | all-reduce | flops 12288 | bytes 98304 | tf_op jit(solution)/shard_map/psum | solution.py:52
  29.7 0.7 convert_select_fusion
  30.5 0.7 broadcast_subtract_fusion
  31.2 3.3 %while.52 = (s32[]{:T(128)}, f32[4,256]{1,0:T(4,128)S(1)}, f32[4,4096]{1,0:T(4,128)S(1)}, s32[4096]{0:T(1024)S(1)}, s32[]{:T(128)}, /*index=5*/s32[]{:T(128)}, s32[]{:T(128)}, s32[]{:T(128)}) while((s32[]{:T(128)}, f32[4,256]{1,0:T(4,128)S(1)}, f32[4,4096]{1,0:T(4,128)S(1)}, s32[4096]{0:T(1024)S(1)}, s32[]{:T(128)}, ...), condition=%wide.region_4.0_spmd.clone, body=%wide.region_3.0_spmd.clone.sunk | while | flops 6424583 | bytes 22677 | solution.py:34
  31.3 0.3 convolution_add_fusion.6
  31.6 0.1 dynamic_slice.84
  31.7 0.3 convolution_add_fusion.6
  32.0 0.1 dynamic_slice.84
  32.1 0.3 convolution_add_fusion.6
  32.4 0.1 dynamic_slice.84
  32.5 0.3 convolution_add_fusion.6
  32.8 0.1 dynamic_slice.84
  32.9 0.3 convolution_add_fusion.6
  33.2 0.1 dynamic_slice.84
  33.4 0.3 convolution_add_fusion.6
  33.7 0.1 dynamic_slice.84
  33.8 0.3 convolution_add_fusion.6
  34.1 0.1 dynamic_slice.84
  34.2 0.3 convolution_add_fusion.6
  34.5 21.6 %psum.22 = f32[4,256]{1,0:T(4,128)S(1)} all-reduce(f32[4,256]{1,0:T(4,128)S(1)} %get-tuple-element.348), channel_id=1, replica_groups=mesh['tm'=2,'loan'=8,'cov'=2] {'loan'}, use_global_device_ids=true, to_apply=%region_5.0 | all-reduce | flops 1024 | bytes 8192 | tf_op jit(solution)/shard_map/psum | solution.py:74
  56.1 0.1 slice_reduce_fusion
  56.2 1.3 %dynamic-slice = u32[1]{0:T(128)} dynamic-slice(u32[32]{0:T(128)} %constant.125, u32[]{:T(128)S(6)} %add.130), dynamic_slice_sizes={1} | dynamic-slice | bytes 12
  58.2 0.2 dynamic-update-slice
  58.5 2.4 %all-reduce = f32[6]{0:T(128)S(1)} all-reduce(f32[6]{0:T(128)S(1)} %dynamic-update-slice), channel_id=2, replica_groups=mesh['tm'=2,'loan'=8,'cov'=2] {'tm'}, use_global_device_ids=true, to_apply=%add | all-reduce | flops 6 | bytes 48
  61.0 0.1 convolution_add_fusion.3
  61.2 0.1 fusion.21
  61.3 0.2 dynamic-update-slice.1
  61.6 2.4 %all-reduce.1 = f32[6]{0:T(128)S(1)} all-reduce(f32[6]{0:T(128)S(1)} %dynamic-update-slice.1), channel_id=3, replica_groups=mesh['tm'=2,'loan'=8,'cov'=2] {'tm'}, use_global_device_ids=true, to_apply=%add.1 | all-reduce | flops 6 | bytes 48
  64.0 0.2 convolution_add_fusion.2
  64.3 19.3 %while.53 = (s32[]{:T(128)}, f32[2,512]{1,0:T(2,128)S(1)}, f32[4096]{0:T(1024)S(1)}, f32[2,4096]{1,0:T(2,128)S(1)}, s32[4096]{0:T(1024)S(1)}, /*index=5*/f32[3,2...) while((s32[]{:T(128)}, f32[2,512]{1,0:T(2,128)S(1)}, ...), condition=%wide.region_9.10_spmd.clone, body=%wide.region_8.9_spmd.clone.sunk | while | flops 11146247 | bytes 1094316 | solution.py:34
  64.4 0.4 convolution_bitcast_fusion.3
  64.8 0.1 dynamic_slice.88
  64.9 1.9 %convolution_add_fusion.7 = f32[2,512]{1,0:T(2,128)S(1)} fusion(f32[4096,512]{1,0:T(8,128)} %get-tuple-element.599, s32[]{:T(128)S(6)} %select_n.79, f32[3,512]{1,0:T(4,128)S(1)} %convolution_bitcast_fusion.3, f32[2,512]{1,0:T(2,128)S(1)} %get-tuple-element.583, f32[2,4096]{1,0:T(2,128)S(1)} %get-tuple-element.596, pred[]{:T(512)S(6)} %compare.7, ...), kind=kOutput, calls=%fused_computation.12.clone.1 | convolution fusion | flops 6296576 | bytes 1070592 | tf_op jit(solution)/shard_map/while/body/eval_jaxpr/dot_general | solution.py:96
  66.8 0.4 convolution_bitcast_fusion.3
  67.2 0.1 dynamic_slice.88
  67.3 1.9 %convolution_add_fusion.7 = f32[2,512]{1,0:T(2,128)S(1)} fusion(f32[4096,512]{1,0:T(8,128)} %get-tuple-element.599, s32[]{:T(128)S(6)} %select_n.79, f32[3,512]{1,0:T(4,128)S(1)} %convolution_bitcast_fusion.3, f32[2,512]{1,0:T(2,128)S(1)} %get-tuple-element.583, f32[2,4096]{1,0:T(2,128)S(1)} %get-tuple-element.596, pred[]{:T(512)S(6)} %compare.7, ...), kind=kOutput, calls=%fused_computation.12.clone.1 | convolution fusion | flops 6296576 | bytes 1070592 | tf_op jit(solution)/shard_map/while/body/eval_jaxpr/dot_general | solution.py:96
  69.2 0.4 convolution_bitcast_fusion.3
  69.7 1.9 %convolution_add_fusion.7 = f32[2,512]{1,0:T(2,128)S(1)} fusion(f32[4096,512]{1,0:T(8,128)} %get-tuple-element.599, s32[]{:T(128)S(6)} %select_n.79, f32[3,512]{1,0:T(4,128)S(1)} %convolution_bitcast_fusion.3, f32[2,512]{1,0:T(2,128)S(1)} %get-tuple-element.583, f32[2,4096]{1,0:T(2,128)S(1)} %get-tuple-element.596, pred[]{:T(512)S(6)} %compare.7, ...), kind=kOutput, calls=%fused_computation.12.clone.1 | convolution fusion | flops 6296576 | bytes 1070592 | tf_op jit(solution)/shard_map/while/body/eval_jaxpr/dot_general | solution.py:96
  71.6 0.4 convolution_bitcast_fusion.3
  72.0 0.1 dynamic_slice.88
  72.1 1.9 %convolution_add_fusion.7 = f32[2,512]{1,0:T(2,128)S(1)} fusion(f32[4096,512]{1,0:T(8,128)} %get-tuple-element.599, s32[]{:T(128)S(6)} %select_n.79, f32[3,512]{1,0:T(4,128)S(1)} %convolution_bitcast_fusion.3, f32[2,512]{1,0:T(2,128)S(1)} %get-tuple-element.583, f32[2,4096]{1,0:T(2,128)S(1)} %get-tuple-element.596, pred[]{:T(512)S(6)} %compare.7, ...), kind=kOutput, calls=%fused_computation.12.clone.1 | convolution fusion | flops 6296576 | bytes 1070592 | tf_op jit(solution)/shard_map/while/body/eval_jaxpr/dot_general | solution.py:96
  74.0 0.4 convolution_bitcast_fusion.3
  74.5 1.9 %convolution_add_fusion.7 = f32[2,512]{1,0:T(2,128)S(1)} fusion(f32[4096,512]{1,0:T(8,128)} %get-tuple-element.599, s32[]{:T(128)S(6)} %select_n.79, f32[3,512]{1,0:T(4,128)S(1)} %convolution_bitcast_fusion.3, f32[2,512]{1,0:T(2,128)S(1)} %get-tuple-element.583, f32[2,4096]{1,0:T(2,128)S(1)} %get-tuple-element.596, pred[]{:T(512)S(6)} %compare.7, ...), kind=kOutput, calls=%fused_computation.12.clone.1 | convolution fusion | flops 6296576 | bytes 1070592 | tf_op jit(solution)/shard_map/while/body/eval_jaxpr/dot_general | solution.py:96
  76.4 0.4 convolution_bitcast_fusion.3
  76.8 0.1 dynamic_slice.88
  76.9 1.9 %convolution_add_fusion.7 = f32[2,512]{1,0:T(2,128)S(1)} fusion(f32[4096,512]{1,0:T(8,128)} %get-tuple-element.599, s32[]{:T(128)S(6)} %select_n.79, f32[3,512]{1,0:T(4,128)S(1)} %convolution_bitcast_fusion.3, f32[2,512]{1,0:T(2,128)S(1)} %get-tuple-element.583, f32[2,4096]{1,0:T(2,128)S(1)} %get-tuple-element.596, pred[]{:T(512)S(6)} %compare.7, ...), kind=kOutput, calls=%fused_computation.12.clone.1 | convolution fusion | flops 6296576 | bytes 1070592 | tf_op jit(solution)/shard_map/while/body/eval_jaxpr/dot_general | solution.py:96
  78.8 0.4 convolution_bitcast_fusion.3
  79.2 0.1 dynamic_slice.88
  79.3 1.9 %convolution_add_fusion.7 = f32[2,512]{1,0:T(2,128)S(1)} fusion(f32[4096,512]{1,0:T(8,128)} %get-tuple-element.599, s32[]{:T(128)S(6)} %select_n.79, f32[3,512]{1,0:T(4,128)S(1)} %convolution_bitcast_fusion.3, f32[2,512]{1,0:T(2,128)S(1)} %get-tuple-element.583, f32[2,4096]{1,0:T(2,128)S(1)} %get-tuple-element.596, pred[]{:T(512)S(6)} %compare.7, ...), kind=kOutput, calls=%fused_computation.12.clone.1 | convolution fusion | flops 6296576 | bytes 1070592 | tf_op jit(solution)/shard_map/while/body/eval_jaxpr/dot_general | solution.py:96
  81.3 0.4 convolution_bitcast_fusion.3
  81.6 0.1 dynamic_slice.88
  81.7 1.9 %convolution_add_fusion.7 = f32[2,512]{1,0:T(2,128)S(1)} fusion(f32[4096,512]{1,0:T(8,128)} %get-tuple-element.599, s32[]{:T(128)S(6)} %select_n.79, f32[3,512]{1,0:T(4,128)S(1)} %convolution_bitcast_fusion.3, f32[2,512]{1,0:T(2,128)S(1)} %get-tuple-element.583, f32[2,4096]{1,0:T(2,128)S(1)} %get-tuple-element.596, pred[]{:T(512)S(6)} %compare.7, ...), kind=kOutput, calls=%fused_computation.12.clone.1 | convolution fusion | flops 6296576 | bytes 1070592 | tf_op jit(solution)/shard_map/while/body/eval_jaxpr/dot_general | solution.py:96
  83.6 29.5 %psum.23 = f32[2,512]{1,0:T(2,128)S(1)} all-reduce(f32[2,512]{1,0:T(2,128)S(1)} %get-tuple-element.349), channel_id=1, replica_groups=mesh['tm'=2,'loan'=8,'cov'=2] {'tm','loan'}, use_global_device_ids=true, to_apply=%region_10.11 | all-reduce | flops 1024 | bytes 8192 | tf_op jit(solution)/shard_map/psum | solution.py:99
  113.1 0.6 broadcast_multiply_fusion.1
  (32 shorter events, 1.3 us)
where the time goes:
time: 115 us; the launch traced here: 114 us
  blocking collectives  66.4 us (58%)
  matrix products  38.3 us (33%)
  local copies, waits for them, and re-layouts  4.14 us (4%)
  other arithmetic  3.32 us (3%)
  between operations  1.43 us (1%)
    psum x1, blocking collectives, per_device(): product = lax.psum(parts, ('tm', 'loan'))  29.5 us
    psum x1, blocking collectives, per_device(): totals = lax.psum(stats_local, 'loan')  21.6 us
    dot_general x8, matrix products, predict(): lax.dot_general(coeffs, piece, (((1,), (1,)), ((), ())), precision=exact_...  17.7 us
    dot_general x8, matrix products, assemble(): return product_acc + jnp.dot(resid, piece, precision=exact_mode)  14.8 us
    psum x1, blocking collectives, per_device(): linear = lax.psum(partial_value, 'cov')  10.4 us
    unnamed x2, blocking collectives  4.89 us
    dot_general x8, matrix products, assemble(): lax.dot_general(cumulative, member, (((1,), (1,)), ((), ())), precision=e...  2.98 us
    dot_general x8, matrix products, tally(): return stats_acc + jnp.dot(values, member, precision=exact_mode)  2.45 us

commit v1 on v0

--- a/solution.py
+++ b/solution.py
@@ -49,7 +49,7 @@
         return lax.dynamic_update_slice_in_dim(partial_value, values, start, 1)
 
     partial_value = sweep(trips, block, predict, jnp.zeros((3, row_total), jnp.float32))
-    linear = lax.psum(partial_value, "cov")
+    linear = jnp.sum(jax.lax.all_gather(partial_value, "cov"), 0)
     valid = (jnp.arange(row_total, dtype=jnp.int32) < row_count).astype(jnp.float32)
     weight = valid * jnp.exp(linear[0])
     projected = linear[1:3]

time: 115 us -> 111 us (0.965)
  blocking collectives: 66.4 us -> 62.5 us
    psum x1 -> x0, blocking collectives: 10.4 us -> none  [per_device(): linear = lax.psum(partial_value, 'cov')]
    all_gather x0 -> x1, blocking collectives: none -> 5.87 us  [per_device(): linear = jnp.sum(jax.lax.all_gather(partial_value, 'cov'), 0)]
where the time goes in v1:
time: 111 us; the launch traced here: 110 us
  blocking collectives  62.5 us (56%)
  matrix products  38.3 us (35%)
  local copies, waits for them, and re-layouts  4.14 us (4%)
  other arithmetic  3.36 us (3%)
  between operations  1.43 us (1%)
    psum x1, blocking collectives, per_device(): product = lax.psum(parts, ('tm', 'loan'))  29.5 us
    psum x1, blocking collectives, per_device(): totals = lax.psum(stats_local, 'loan')  22.3 us
    dot_general x8, matrix products, predict(): lax.dot_general(coeffs, piece, (((1,), (1,)), ((), ())), precision=exact_...  17.7 us
    dot_general x8, matrix products, assemble(): return product_acc + jnp.dot(resid, piece, precision=exact_mode)  14.8 us
    all_gather x1, blocking collectives, per_device(): linear = jnp.sum(jax.lax.all_gather(partial_value, 'cov'), 0)  5.87 us
    unnamed x2, blocking collectives  4.89 us
    dot_general x8, matrix products, assemble(): lax.dot_general(cumulative, member, (((1,), (1,)), ((), ())), precision=e...  2.98 us
    dot_general x8, matrix products, tally(): return stats_acc + jnp.dot(values, member, precision=exact_mode)  2.45 us

profile of v1, /device:TPU:0, one launch (start us, length us, event | category | flops | bytes accessed | tf_op | source)
XLA Modules:
  0.0 109.8 jit_solution(14468728578998467763)
XLA Ops:
  0.7 0.7 pad_maximum_fusion.1
  1.4 17.8 %while.51 = (s32[]{:T(128)}, f32[3,4096]{1,0:T(4,128)S(1)}, f32[4096,512]{1,0:T(8,128)}, f32[3,512]{1,0:T(4,128)S(1)}, s32[]{:T(128)}, /*index=5*/s32[]{:T(128)}, s32[]{:T(128)}, s32[]{:T(128)}) while((s32[]{:T(128)}, f32[3,4096]{1,0:T(4,128)S(1)}, f32[4096,512]{1,0:T(8,128)}, f32[3,512]{1,0:T(4,128)S(1)}, s32[]{:T(128)}, ...), condition=%wide.region_1.0_spmd, body=%wide.region_0.0_spmd.sunk | while | flops 9437190 | bytes 1066115 | solution.py:34
  1.4 2.2 %fusion.35 = f32[3,4096]{1,0:T(4,128)S(1)} fusion(f32[3,4096]{1,0:T(4,128)S(1)} %get-tuple-element.532, s32[]{:T(128)S(6)} %select_n.77, f32[3,512]{1,0:T(4,128)S(1)} %get-tuple-element.542, f32[4096,512]{1,0:T(8,128)} %get-tuple-element.541), kind=kOutput, calls=%fused_computation.3.clone.1 | convolution fusion | flops 9437184 | bytes 1065984 | tf_op jit(solution)/shard_map/while/body/eval_jaxpr/dot_general | solution.py:48
  3.6 2.2 %fusion.35 = f32[3,4096]{1,0:T(4,128)S(1)} fusion(f32[3,4096]{1,0:T(4,128)S(1)} %get-tuple-element.532, s32[]{:T(128)S(6)} %select_n.77, f32[3,512]{1,0:T(4,128)S(1)} %get-tuple-element.542, f32[4096,512]{1,0:T(8,128)} %get-tuple-element.541), kind=kOutput, calls=%fused_computation.3.clone.1 | convolution fusion | flops 9437184 | bytes 1065984 | tf_op jit(solution)/shard_map/while/body/eval_jaxpr/dot_general | solution.py:48
  5.8 2.2 %fusion.35 = f32[3,4096]{1,0:T(4,128)S(1)} fusion(f32[3,4096]{1,0:T(4,128)S(1)} %get-tuple-element.532, s32[]{:T(128)S(6)} %select_n.77, f32[3,512]{1,0:T(4,128)S(1)} %get-tuple-element.542, f32[4096,512]{1,0:T(8,128)} %get-tuple-element.541), kind=kOutput, calls=%fused_computation.3.clone.1 | convolution fusion | flops 9437184 | bytes 1065984 | tf_op jit(solution)/shard_map/while/body/eval_jaxpr/dot_general | solution.py:48
  8.0 2.2 %fusion.35 = f32[3,4096]{1,0:T(4,128)S(1)} fusion(f32[3,4096]{1,0:T(4,128)S(1)} %get-tuple-element.532, s32[]{:T(128)S(6)} %select_n.77, f32[3,512]{1,0:T(4,128)S(1)} %get-tuple-element.542, f32[4096,512]{1,0:T(8,128)} %get-tuple-element.541), kind=kOutput, calls=%fused_computation.3.clone.1 | convolution fusion | flops 9437184 | bytes 1065984 | tf_op jit(solution)/shard_map/while/body/eval_jaxpr/dot_general | solution.py:48
  10.3 2.2 %fusion.35 = f32[3,4096]{1,0:T(4,128)S(1)} fusion(f32[3,4096]{1,0:T(4,128)S(1)} %get-tuple-element.532, s32[]{:T(128)S(6)} %select_n.77, f32[3,512]{1,0:T(4,128)S(1)} %get-tuple-element.542, f32[4096,512]{1,0:T(8,128)} %get-tuple-element.541), kind=kOutput, calls=%fused_computation.3.clone.1 | convolution fusion | flops 9437184 | bytes 1065984 | tf_op jit(solution)/shard_map/while/body/eval_jaxpr/dot_general | solution.py:48
  12.5 2.2 %fusion.35 = f32[3,4096]{1,0:T(4,128)S(1)} fusion(f32[3,4096]{1,0:T(4,128)S(1)} %get-tuple-element.532, s32[]{:T(128)S(6)} %select_n.77, f32[3,512]{1,0:T(4,128)S(1)} %get-tuple-element.542, f32[4096,512]{1,0:T(8,128)} %get-tuple-element.541), kind=kOutput, calls=%fused_computation.3.clone.1 | convolution fusion | flops 9437184 | bytes 1065984 | tf_op jit(solution)/shard_map/while/body/eval_jaxpr/dot_general | solution.py:48
  14.7 2.2 %fusion.35 = f32[3,4096]{1,0:T(4,128)S(1)} fusion(f32[3,4096]{1,0:T(4,128)S(1)} %get-tuple-element.532, s32[]{:T(128)S(6)} %select_n.77, f32[3,512]{1,0:T(4,128)S(1)} %get-tuple-element.542, f32[4096,512]{1,0:T(8,128)} %get-tuple-element.541), kind=kOutput, calls=%fused_computation.3.clone.1 | convolution fusion | flops 9437184 | bytes 1065984 | tf_op jit(solution)/shard_map/while/body/eval_jaxpr/dot_general | solution.py:48
  16.9 2.2 %fusion.35 = f32[3,4096]{1,0:T(4,128)S(1)} fusion(f32[3,4096]{1,0:T(4,128)S(1)} %get-tuple-element.532, s32[]{:T(128)S(6)} %select_n.77, f32[3,512]{1,0:T(4,128)S(1)} %get-tuple-element.542, f32[4096,512]{1,0:T(8,128)} %get-tuple-element.541), kind=kOutput, calls=%fused_computation.3.clone.1 | convolution fusion | flops 9437184 | bytes 1065984 | tf_op jit(solution)/shard_map/while/body/eval_jaxpr/dot_general | solution.py:48
  19.1 5.9 %all-gather.3 = f32[2,3,4096]{2,1,0:T(4,128)S(1)} all-gather(f32[1,3,4096]{2,1,0:T(4,128)S(1)} %bitcast.31), channel_id=2, replica_groups=mesh['tm'=2,'loan'=8,'cov'=2] {'cov'}, dimensions={0}, use_global_device_ids=true | all-gather | bytes 147456 | tf_op jit(solution)/shard_map/all_gather | solution.py:52
  25.1 0.7 convert_select_fusion
  25.9 0.7 broadcast_subtract_fusion
  26.6 3.3 %while.52 = (s32[]{:T(128)}, f32[4,256]{1,0:T(4,128)S(1)}, f32[4,4096]{1,0:T(4,128)S(1)}, s32[4096]{0:T(1024)S(1)}, s32[]{:T(128)}, /*index=5*/s32[]{:T(128)}, s32[]{:T(128)}, s32[]{:T(128)}) while((s32[]{:T(128)}, f32[4,256]{1,0:T(4,128)S(1)}, f32[4,4096]{1,0:T(4,128)S(1)}, s32[4096]{0:T(1024)S(1)}, s32[]{:T(128)}, ...), condition=%wide.region_4.0_spmd.clone, body=%wide.region_3.0_spmd.clone.sunk | while | flops 6424583 | bytes 22677 | solution.py:34
  26.7 0.3 convolution_add_fusion.6
  27.0 0.1 dynamic_slice.84
  27.1 0.3 convolution_add_fusion.6
  27.4 0.1 dynamic_slice.84
  27.5 0.3 convolution_add_fusion.6
  27.9 0.1 dynamic_slice.84
  28.0 0.3 convolution_add_fusion.6
  28.3 0.1 dynamic_slice.84
  28.4 0.3 convolution_add_fusion.6
  28.7 0.1 dynamic_slice.84
  28.8 0.3 convolution_add_fusion.6
  29.1 0.1 dynamic_slice.84
  29.2 0.3 convolution_add_fusion.6
  29.5 0.1 dynamic_slice.84
  29.7 0.3 convolution_add_fusion.6
  30.0 22.3 %psum.14 = f32[4,256]{1,0:T(4,128)S(1)} all-reduce(f32[4,256]{1,0:T(4,128)S(1)} %get-tuple-element.348), channel_id=1, replica_groups=mesh['tm'=2,'loan'=8,'cov'=2] {'loan'}, use_global_device_ids=true, to_apply=%region_5.0 | all-reduce | flops 1024 | bytes 8192 | tf_op jit(solution)/shard_map/psum | solution.py:74
  52.2 0.1 slice_reduce_fusion
  52.3 1.3 %dynamic-slice = u32[1]{0:T(128)} dynamic-slice(u32[32]{0:T(128)} %constant.125, u32[]{:T(128)S(6)} %add.128), dynamic_slice_sizes={1} | dynamic-slice | bytes 12
  54.4 0.2 dynamic-update-slice
  54.6 2.4 %all-reduce = f32[6]{0:T(128)S(1)} all-reduce(f32[6]{0:T(128)S(1)} %dynamic-update-slice), channel_id=3, replica_groups=mesh['tm'=2,'loan'=8,'cov'=2] {'tm'}, use_global_device_ids=true, to_apply=%add | all-reduce | flops 6 | bytes 48
  57.1 0.1 convolution_add_fusion.3
  57.4 0.1 fusion.21
  57.5 0.2 dynamic-update-slice.1
  57.7 2.4 %all-reduce.1 = f32[6]{0:T(128)S(1)} all-reduce(f32[6]{0:T(128)S(1)} %dynamic-update-slice.1), channel_id=4, replica_groups=mesh['tm'=2,'loan'=8,'cov'=2] {'tm'}, use_global_device_ids=true, to_apply=%add.1 | all-reduce | flops 6 | bytes 48
  60.2 0.2 convolution_add_fusion.2
  60.5 19.3 %while.53 = (s32[]{:T(128)}, f32[2,512]{1,0:T(2,128)S(1)}, f32[4096]{0:T(1024)S(1)}, f32[2,4096]{1,0:T(2,128)S(1)}, s32[4096]{0:T(1024)S(1)}, /*index=5*/f32[3,2...) while((s32[]{:T(128)}, f32[2,512]{1,0:T(2,128)S(1)}, ...), condition=%wide.region_9.10_spmd.clone, body=%wide.region_8.9_spmd.clone.sunk | while | flops 11146247 | bytes 1094316 | solution.py:34
  60.5 0.4 convolution_bitcast_fusion.3
  61.0 1.9 %convolution_add_fusion.7 = f32[2,512]{1,0:T(2,128)S(1)} fusion(f32[4096,512]{1,0:T(8,128)} %get-tuple-element.599, s32[]{:T(128)S(6)} %select_n.79, f32[3,512]{1,0:T(4,128)S(1)} %convolution_bitcast_fusion.3, f32[2,512]{1,0:T(2,128)S(1)} %get-tuple-element.583, f32[2,4096]{1,0:T(2,128)S(1)} %get-tuple-element.596, pred[]{:T(512)S(6)} %compare.7, ...), kind=kOutput, calls=%fused_computation.12.clone.1 | convolution fusion | flops 6296576 | bytes 1070592 | tf_op jit(solution)/shard_map/while/body/eval_jaxpr/dot_general | solution.py:96
  63.0 0.4 convolution_bitcast_fusion.3
  63.3 0.1 dynamic_slice.88
  63.4 1.9 %convolution_add_fusion.7 = f32[2,512]{1,0:T(2,128)S(1)} fusion(f32[4096,512]{1,0:T(8,128)} %get-tuple-element.599, s32[]{:T(128)S(6)} %select_n.79, f32[3,512]{1,0:T(4,128)S(1)} %convolution_bitcast_fusion.3, f32[2,512]{1,0:T(2,128)S(1)} %get-tuple-element.583, f32[2,4096]{1,0:T(2,128)S(1)} %get-tuple-element.596, pred[]{:T(512)S(6)} %compare.7, ...), kind=kOutput, calls=%fused_computation.12.clone.1 | convolution fusion | flops 6296576 | bytes 1070592 | tf_op jit(solution)/shard_map/while/body/eval_jaxpr/dot_general | solution.py:96
  65.4 0.4 convolution_bitcast_fusion.3
  65.7 0.1 dynamic_slice.88
  65.8 1.9 %convolution_add_fusion.7 = f32[2,512]{1,0:T(2,128)S(1)} fusion(f32[4096,512]{1,0:T(8,128)} %get-tuple-element.599, s32[]{:T(128)S(6)} %select_n.79, f32[3,512]{1,0:T(4,128)S(1)} %convolution_bitcast_fusion.3, f32[2,512]{1,0:T(2,128)S(1)} %get-tuple-element.583, f32[2,4096]{1,0:T(2,128)S(1)} %get-tuple-element.596, pred[]{:T(512)S(6)} %compare.7, ...), kind=kOutput, calls=%fused_computation.12.clone.1 | convolution fusion | flops 6296576 | bytes 1070592 | tf_op jit(solution)/shard_map/while/body/eval_jaxpr/dot_general | solution.py:96
  67.8 0.4 convolution_bitcast_fusion.3
  68.2 0.1 dynamic_slice.88
  68.3 1.9 %convolution_add_fusion.7 = f32[2,512]{1,0:T(2,128)S(1)} fusion(f32[4096,512]{1,0:T(8,128)} %get-tuple-element.599, s32[]{:T(128)S(6)} %select_n.79, f32[3,512]{1,0:T(4,128)S(1)} %convolution_bitcast_fusion.3, f32[2,512]{1,0:T(2,128)S(1)} %get-tuple-element.583, f32[2,4096]{1,0:T(2,128)S(1)} %get-tuple-element.596, pred[]{:T(512)S(6)} %compare.7, ...), kind=kOutput, calls=%fused_computation.12.clone.1 | convolution fusion | flops 6296576 | bytes 1070592 | tf_op jit(solution)/shard_map/while/body/eval_jaxpr/dot_general | solution.py:96
  70.2 0.4 convolution_bitcast_fusion.3
  70.6 0.1 dynamic_slice.88
  70.7 1.9 %convolution_add_fusion.7 = f32[2,512]{1,0:T(2,128)S(1)} fusion(f32[4096,512]{1,0:T(8,128)} %get-tuple-element.599, s32[]{:T(128)S(6)} %select_n.79, f32[3,512]{1,0:T(4,128)S(1)} %convolution_bitcast_fusion.3, f32[2,512]{1,0:T(2,128)S(1)} %get-tuple-element.583, f32[2,4096]{1,0:T(2,128)S(1)} %get-tuple-element.596, pred[]{:T(512)S(6)} %compare.7, ...), kind=kOutput, calls=%fused_computation.12.clone.1 | convolution fusion | flops 6296576 | bytes 1070592 | tf_op jit(solution)/shard_map/while/body/eval_jaxpr/dot_general | solution.py:96
  72.6 0.4 convolution_bitcast_fusion.3
  73.1 1.9 %convolution_add_fusion.7 = f32[2,512]{1,0:T(2,128)S(1)} fusion(f32[4096,512]{1,0:T(8,128)} %get-tuple-element.599, s32[]{:T(128)S(6)} %select_n.79, f32[3,512]{1,0:T(4,128)S(1)} %convolution_bitcast_fusion.3, f32[2,512]{1,0:T(2,128)S(1)} %get-tuple-element.583, f32[2,4096]{1,0:T(2,128)S(1)} %get-tuple-element.596, pred[]{:T(512)S(6)} %compare.7, ...), kind=kOutput, calls=%fused_computation.12.clone.1 | convolution fusion | flops 6296576 | bytes 1070592 | tf_op jit(solution)/shard_map/while/body/eval_jaxpr/dot_general | solution.py:96
  75.0 0.4 convolution_bitcast_fusion.3
  75.4 0.1 dynamic_slice.88
  75.5 1.9 %convolution_add_fusion.7 = f32[2,512]{1,0:T(2,128)S(1)} fusion(f32[4096,512]{1,0:T(8,128)} %get-tuple-element.599, s32[]{:T(128)S(6)} %select_n.79, f32[3,512]{1,0:T(4,128)S(1)} %convolution_bitcast_fusion.3, f32[2,512]{1,0:T(2,128)S(1)} %get-tuple-element.583, f32[2,4096]{1,0:T(2,128)S(1)} %get-tuple-element.596, pred[]{:T(512)S(6)} %compare.7, ...), kind=kOutput, calls=%fused_computation.12.clone.1 | convolution fusion | flops 6296576 | bytes 1070592 | tf_op jit(solution)/shard_map/while/body/eval_jaxpr/dot_general | solution.py:96
  77.4 0.4 convolution_bitcast_fusion.3
  77.8 0.1 dynamic_slice.88
  77.9 1.9 %convolution_add_fusion.7 = f32[2,512]{1,0:T(2,128)S(1)} fusion(f32[4096,512]{1,0:T(8,128)} %get-tuple-element.599, s32[]{:T(128)S(6)} %select_n.79, f32[3,512]{1,0:T(4,128)S(1)} %convolution_bitcast_fusion.3, f32[2,512]{1,0:T(2,128)S(1)} %get-tuple-element.583, f32[2,4096]{1,0:T(2,128)S(1)} %get-tuple-element.596, pred[]{:T(512)S(6)} %compare.7, ...), kind=kOutput, calls=%fused_computation.12.clone.1 | convolution fusion | flops 6296576 | bytes 1070592 | tf_op jit(solution)/shard_map/while/body/eval_jaxpr/dot_general | solution.py:96
  79.7 29.5 %psum.15 = f32[2,512]{1,0:T(2,128)S(1)} all-reduce(f32[2,512]{1,0:T(2,128)S(1)} %get-tuple-element.349), channel_id=1, replica_groups=mesh['tm'=2,'loan'=8,'cov'=2] {'tm','loan'}, use_global_device_ids=true, to_apply=%region_10.11 | all-reduce | flops 1024 | bytes 8192 | tf_op jit(solution)/shard_map/psum | solution.py:99
  109.2 0.6 broadcast_multiply_fusion.1
  (33 shorter events, 1.3 us)
